TPU v7x, 128 devices: a whole 4x4x4 slice. The times are simulated.
128 devices in a mesh: row: 8 (over z_hi, y), col: 16 (over z_lo, x, core).
Axes of the slice: x: 4, y: 4, z: 4 (z_hi: 2, z_lo: 2; z = z_hi * 2 + z_lo), core: 2. Of those that a mesh axis runs over, the one named last changes fastest.
Arguments:
- gram: float32 [8192, 8192], P('row', 'col'), may hold values from -6 to 8
- rotations: float32 [2, 8, 1024, 1024], P(None, 'row', 'col'), may hold values from -1 to 2
Outputs:
- rotated: float32 [8192, 8192], P('row', 'col')
All inputs are finite; a program needn't handle non-finite values.
Results may differ from a plain program's by a relative error of at most 0.00016.
Values sent between devices are 32-bit elements; how exact they have to be, the bound alone decides.
No kernel may reach another device: no remote copies, remote signals or barrier semaphores. Data moves between devices by JAX's collectives and lax.ppermute only.
A program may use at most 64 MiB of HBM per device.

v0:
```python
import jax
import jax.numpy as jnp
from jax import lax
from jax.experimental import pallas as pl
from jax.experimental.pallas import tpu as pltpu
from jax.sharding import PartitionSpec as P


N = 512
F32 = jnp.float32
HIGH = lax.Precision.HIGH


def place(index):
    row, col = divmod(index, 16)
    return (row // 4, row % 4, col // 8, (col // 2) % 4, col % 2)


def index_of(z_hi, y, z_lo, x, core):
    return (z_hi * 4 + y % 4) * 16 + z_lo * 8 + (x % 4) * 2 + core


def pairs_of(move):
    return [(i, index_of(*move(*place(i)))) for i in range(128)]


def along_x(step):
    return pairs_of(lambda zh, y, zl, x, c: (zh, y, zl, x + step, c))


def along_y(step):
    return pairs_of(lambda zh, y, zl, x, c: (zh, y + step, zl, x, c))


OTHER_LO = pairs_of(lambda zh, y, zl, x, c: (zh, y, 1 - zl, x, c))
OTHER_HI = pairs_of(lambda zh, y, zl, x, c: (1 - zh, y, zl, x, c))
OTHER_CORE = pairs_of(lambda zh, y, zl, x, c: (zh, y, zl, x, 1 - c))
TRANSPOSE = pairs_of(lambda zh, y, zl, x, c: (zl, x, zh, y, c))


def new_position(old):
    if old == 0:
        return 0
    if old == 1:
        return 2
    if old == 14:
        return 15
    return old + 2 if old % 2 == 0 else old - 2


MOVE_COL = [(r * 16 + c, r * 16 + new_position(c)) for r in range(8) for c in range(16)]
ROW_UP = [(r * 16 + c, (r + 1) * 16 + c) for r in range(7) for c in range(16)]
ROW_DOWN = [(r * 16 + c, (r - 1) * 16 + c) for r in range(1, 8) for c in range(16)]


def send(value, pairs):
    return lax.ppermute(value, ("row", "col"), pairs)


def vmem_call(body, inputs, outs):
    return pl.pallas_call(
        body,
        out_shape=[jax.ShapeDtypeStruct(shape, F32) for shape in outs],
        in_specs=[pl.BlockSpec(memory_space=pltpu.VMEM)] * len(inputs),
        out_specs=[pl.BlockSpec(memory_space=pltpu.VMEM)] * len(outs),
        compiler_params=pltpu.CompilerParams(vmem_limit_bytes=12 * 2**20),
        cost_estimate=pl.CostEstimate(flops=0, bytes_accessed=2**22, transcendentals=0),
    )(*inputs)


def rows_body(*refs):
    pieces, out = refs[:8], refs[8]
    col = lax.axis_index("col")
    ring, plane = (col // 2) % 4, col // 8
    for j in range(8):
        at = (plane if j < 4 else 1 - plane) * 4 + (ring + j % 4) % 4
        for half in range(2):
            first = at * 128 + 64 * jnp.where(col % 2 == 0, half, 1 - half)
            rows = pl.ds(pl.multiple_of(first, 64), 64)
            out[rows, :] = pieces[j][half * 64 : half * 64 + 64, :]


def join_body(own, other, out):
    up_is_own = (lax.axis_index("col") % 2 == 0) != (lax.axis_index("row") == 0)

    @pl.when(up_is_own)
    def _():
        out[:, 0:N] = own[...]
        out[:, N:] = other[...]

    @pl.when(jnp.logical_not(up_is_own))
    def _():
        out[:, 0:N] = other[...]
        out[:, N:] = own[...]


def cols_body(*refs):
    pieces, own, other = refs[:8], refs[8], refs[9]
    row, core = lax.axis_index("row"), lax.axis_index("col") % 2
    ring, plane = row % 4, row // 4

    def fill(first, second):
        for j in range(8):
            out = first if j < 4 else second
            for part in range(2):
                at = (ring + j % 4) % 4 * 128 + 64 * jnp.where(core == 0, part, 1 - part)
                rows = pl.ds(pl.multiple_of(at, 64), 64)
                out[rows, :] = pieces[j][part * 64 : part * 64 + 64, :]

    @pl.when(plane == core)
    def _():
        fill(own, other)

    @pl.when(plane != core)
    def _():
        fill(other, own)


def mix(turn, tile):
    dims = (((0,), (0,)), ((), ()))
    return lax.dot_general(turn, tile, dims, precision=HIGH, preferred_element_type=F32)


def times(tile, turn):
    return jnp.dot(tile, turn, precision=HIGH, preferred_element_type=F32)


ROW_RING = (along_x(1), along_x(-1), along_x(2), OTHER_LO)
COL_RING = (along_y(1), along_y(-1), along_y(2), OTHER_HI)


def gather(own, ring):
    forward, backward, opposite, other = ring
    to = lambda value, pairs: send(value, pairs)
    across = to(own, other)
    before = to(own, forward)
    behind = to(own, backward)
    far = to(own, opposite)
    across_before = to(across, forward)
    across_behind = to(across, backward)
    across_far = to(far, other)
    return [own, behind, far, before, across, across_behind, across_far, across_before]


def shards(gram, rotations):
    row = lax.axis_index("row")
    core = lax.axis_index("col") % 2
    keep = lax.dynamic_slice_in_dim(rotations[:, 0], core * N, N, 2)
    give = lax.dynamic_slice_in_dim(rotations[:, 0], (1 - core) * N, N, 2)
    got = send(give, OTHER_CORE)

    def turns(step):
        at = int(step) - 1
        piece = jnp.concatenate([keep[at], got[at]])
        turned = send(piece, TRANSPOSE)
        (half,) = vmem_call(rows_body, gather(piece, ROW_RING), [(2 * N, N)])
        other = send(half, OTHER_CORE)
        (whole,) = vmem_call(join_body, (half, other), [(2 * N, 2 * N)])
        pieces = gather(turned, COL_RING)
        return whole, vmem_call(cols_body, pieces, [(N, N)] * 2)

    def advance(tile, rows, cols):
        own_cols, other_cols = cols
        mixed = mix(rows, tile)
        other = send(mixed, OTHER_CORE)
        own_parts = times(mixed[:N], own_cols), times(mixed[N:], own_cols)
        up, down = lax.optimization_barrier(own_parts)
        up = up + times(other[:N], other_cols)
        down = down + times(other[N:], other_cols)
        up = send(up, MOVE_COL)
        down = send(down, MOVE_COL)
        from_above = send(up, ROW_UP)
        from_below = send(down, ROW_DOWN)
        first = jnp.where(row == 0, down, from_above)
        second = jnp.where(row == 7, up, from_below)
        return jnp.concatenate([first, second])

    tile = gram
    for step in ("1", "2"):
        tile = advance(tile, *turns(step))
    return tile


def solution(mesh):
    placed = (P("row", "col"), P(None, "row", "col", None))
    return jax.shard_map(
        shards, mesh=mesh, in_specs=placed, out_specs=P("row", "col"), check_vma=False
    )
```

profile of v0, /device:TPU:7, one launch (start us, length us, event | category | flops | bytes accessed | tf_op | source)
XLA Modules:
  0.0 279.8 jit_solution(4859723927307342594)
XLA Ops:
  7.8 3.3 %collective-permute-done.12.refs_4_ = f32[128,512]{1,0:T(8,128)S(1)} collective-permute-done((f32[128,512]{1,0:T(8,128)S(1)}, f32[128,512]{1,0:T(8,128)S(1)}, u32[]{:S(2)}, u32[]{:S(2)}) %collective-permute-start.12) | collective-permute-done | bytes 262176 | tf_op jit(solution)/shard_map/ppermute | solution.py:57
  11.6 2.0 collective-permute-done.10.refs_2_
  15.0 2.0 collective-permute-done.11.refs_3_
  17.0 3.2 %collective-permute-done.9.refs_1_ = f32[128,512]{1,0:T(8,128)S(1)} collective-permute-done((f32[128,512]{1,0:T(8,128)S(1)}, f32[128,512]{1,0:T(8,128)S(1)}, u32[]{:S(2)}, u32[]{:S(2)}) %collective-permute-start.9) | collective-permute-done | bytes 262176 | tf_op jit(solution)/shard_map/ppermute | solution.py:57
  20.2 5.6 %collective-permute-done.13.refs_5_ = f32[128,512]{1,0:T(8,128)S(1)} collective-permute-done((f32[128,512]{1,0:T(8,128)S(1)}, f32[128,512]{1,0:T(8,128)S(1)}, u32[]{:S(2)}, u32[]{:S(2)}) %collective-permute-start.13) | collective-permute-done | bytes 262176 | tf_op jit(solution)/shard_map/ppermute | solution.py:57
  26.5 3.8 %collective-permute-done.16.other = f32[1024,512]{1,0:T(8,128)S(1)} collective-permute-done((f32[1024,512]{1,0:T(8,128)S(1)}, f32[1024,512]{1,0:T(8,128)S(1)}, u32[]{:S(2)}, u32[]{:S(2)}) %collective-permute-start.16) | collective-permute-done | bytes 2097184 | tf_op jit(solution)/shard_map/ppermute | solution.py:57
  30.6 3.6 %fusion.17 = f32[1024,512]{1,0:T(8,128)S(1)} fusion(f32[1024,1024]{1,0:T(8,128)S(1)} %shard_map.31, f32[1024,512]{1,0:T(8,128)S(1)} %copy-done), kind=kOutput, calls=%fused_computation.33 | convolution fusion | flops 3221225472 | bytes 8388608 | tf_op jit(solution)/shard_map/dot_general | solution.py:121
  34.6 4.7 %collective-permute-start.17 = (f32[128,512]{1,0:T(8,128)S(1)}, f32[128,512]{1,0:T(8,128)S(1)}, u32[]{:S(2)}, u32[]{:S(2)}) collective-permute-start(f32[128,512]{1,0:T(8,128)S(1)} %pad_maximum_fusion.2.refs_0_), channel_id=1, source_target_pairs={{0,0},{1,1},{2,16},{3,17},{4,32},{5,33},{6,48},{7,49},{8,64},{9,65... | collective-permute-start | bytes 786440 | tf_op jit(solution)/shard_map/ppermute | solution.py:57
  39.3 2.8 collective-permute-start.4
  42.9 15.9 %collective-permute-done.17.refs_0_ = f32[128,512]{1,0:T(8,128)S(1)} collective-permute-done((f32[128,512]{1,0:T(8,128)S(1)}, f32[128,512]{1,0:T(8,128)S(1)}, u32[]{:S(2)}, u32[]{:S(2)}) %collective-permute-start.17) | collective-permute-done | bytes 262176 | tf_op jit(solution)/shard_map/ppermute | solution.py:57
  58.8 4.2 %collective-permute-start.21 = (f32[128,512]{1,0:T(8,128)S(1)}, f32[128,512]{1,0:T(8,128)S(1)}, u32[]{:S(2)}, u32[]{:S(2)}) collective-permute-start(f32[128,512]{1,0:T(8,128)S(1)} %collective-permute-done.17.refs_0_), channel_id=1, source_target_pairs={{0,64},{1,65},{2,66},{3,67},{4,68},{5,69},{6,70},{7,71},{8,72},{9,... | collective-permute-start | bytes 786440 | tf_op jit(solution)/shard_map/ppermute | solution.py:57
  63.0 3.1 %collective-permute-start.18 = (f32[128,512]{1,0:T(8,128)S(1)}, f32[128,512]{1,0:T(8,128)S(1)}, u32[]{:S(2)}, u32[]{:S(2)}) collective-permute-start(f32[128,512]{1,0:T(8,128)S(1)} %collective-permute-done.17.refs_0_), channel_id=1, source_target_pairs={{0,48},{1,49},{2,50},{3,51},{4,52},{5,53},{6,54},{7,55},{8,56},{9,... | collective-permute-start | bytes 786440 | tf_op jit(solution)/shard_map/ppermute | solution.py:57
  68.1 2.4 collective-permute-done.19.refs_2_
  70.5 7.1 %collective-permute-done.18.refs_1_ = f32[128,512]{1,0:T(8,128)S(1)} collective-permute-done((f32[128,512]{1,0:T(8,128)S(1)}, f32[128,512]{1,0:T(8,128)S(1)}, u32[]{:S(2)}, u32[]{:S(2)}) %collective-permute-start.18) | collective-permute-done | bytes 262176 | tf_op jit(solution)/shard_map/ppermute | solution.py:57
  79.0 2.0 collective-permute-start.22
  82.6 3.5 %collective-permute-done.20.refs_3_ = f32[128,512]{1,0:T(8,128)S(1)} collective-permute-done((f32[128,512]{1,0:T(8,128)S(1)}, f32[128,512]{1,0:T(8,128)S(1)}, u32[]{:S(2)}, u32[]{:S(2)}) %collective-permute-start.20) | collective-permute-done | bytes 262176 | tf_op jit(solution)/shard_map/ppermute | solution.py:57
  86.1 3.8 %collective-permute-start.8 = (f32[1024,512]{1,0:T(8,128)}, f32[1024,512]{1,0:T(8,128)}, u32[]{:S(2)}, u32[]{:S(2)}) collective-permute-start(f32[1024,512]{1,0:T(8,128)} %shard_map.28.own), channel_id=1, source_target_pairs={{0,1},{1,0},{2,3},{3,2},{4,5},{5,4},{6,7},{7,6},{8,9},{9,8},{10,11... | collective-permute-start | bytes 6291464 | tf_op jit(solution)/shard_map/ppermute | solution.py:57
  99.8 12.8 %collective-permute-done.27 = f32[512,512]{1,0:T(8,128)S(1)} collective-permute-done((f32[512,512]{1,0:T(8,128)S(1)}, f32[512,512]{1,0:T(8,128)S(1)}, u32[]{:S(2)}, u32[]{:S(2)}) %collective-permute-start.27) | collective-permute-done | bytes 1048608 | tf_op jit(solution)/shard_map/ppermute | solution.py:57
  112.6 3.2 %collective-permute-start.28 = (f32[512,512]{1,0:T(8,128)S(1)}, f32[512,512]{1,0:T(8,128)}, u32[]{:S(2)}, u32[]{:S(2)}) collective-permute-start(f32[512,512]{1,0:T(8,128)S(1)} %collective-permute-done.27), channel_id=1, source_target_pairs={{0,16},{1,17},{2,18},{3,19},{4,20},{5,21},{6,22},{7,23},{8,24},{9,... | collective-permute-start | bytes 3145736 | tf_op jit(solution)/shard_map/ppermute | solution.py:57
  115.8 17.7 %collective-permute-done.26 = f32[512,512]{1,0:T(8,128)} collective-permute-done((f32[512,512]{1,0:T(8,128)S(1)}, f32[512,512]{1,0:T(8,128)}, u32[]{:S(2)}, u32[]{:S(2)}) %collective-permute-start.26) | collective-permute-done | bytes 1048608 | tf_op jit(solution)/shard_map/ppermute | solution.py:57
  134.8 2.5 shard_map.29
  138.7 15.8 %collective-permute-done.29 = f32[512,512]{1,0:T(8,128)} collective-permute-done((f32[512,512]{1,0:T(8,128)}, f32[512,512]{1,0:T(8,128)}, u32[]{:S(2)}, u32[]{:S(2)}) %collective-permute-start.29) | collective-permute-done | bytes 1048608 | tf_op jit(solution)/shard_map/ppermute | solution.py:57
  155.9 3.5 %fusion = f32[1024,512]{1,0:T(8,128)S(1)} fusion(f32[1024,1024]{1,0:T(8,128)S(1)} %shard_map.29, f32[512,512]{1,0:T(8,128)S(1)} %broadcast_select_fusion.1, f32[512,512]{1,0:T(8,128)S(1)} %broadcast_select_fusion.3), kind=kOutput, calls=%fused_computation | convolution fusion | flops 3221749760 | bytes 8388608 | tf_op jit(solution)/shard_map/dot_general | solution.py:121
  159.5 6.8 %collective-permute-start.38 = (f32[1024,512]{1,0:T(8,128)S(1)}, f32[1024,512]{1,0:T(8,128)S(1)}, u32[]{:S(2)}, u32[]{:S(2)}) collective-permute-start(f32[1024,512]{1,0:T(8,128)S(1)} %fusion), channel_id=1, source_target_pairs={{0,1},{1,0},{2,3},{3,2},{4,5},{5,4},{6,7},{7,6},{8,9},{9,8},{10,11... | collective-permute-start | bytes 6291464 | tf_op jit(solution)/shard_map/ppermute | solution.py:57
  168.2 16.5 %collective-permute-done.30.refs_0_ = f32[128,512]{1,0:T(8,128)S(1)} collective-permute-done((f32[128,512]{1,0:T(8,128)S(1)}, f32[128,512]{1,0:T(8,128)S(1)}, u32[]{:S(2)}, u32[]{:S(2)}) %collective-permute-start.30) | collective-permute-done | bytes 262176 | tf_op jit(solution)/shard_map/ppermute | solution.py:57
  186.1 7.5 %collective-permute-done.34.refs_4_ = f32[128,512]{1,0:T(8,128)S(1)} collective-permute-done((f32[128,512]{1,0:T(8,128)S(1)}, f32[128,512]{1,0:T(8,128)S(1)}, u32[]{:S(2)}, u32[]{:S(2)}) %collective-permute-start.34) | collective-permute-done | bytes 262176 | tf_op jit(solution)/shard_map/ppermute | solution.py:57
  193.6 2.7 collective-permute-start.36
  196.3 3.7 %collective-permute-done.33.refs_3_ = f32[128,512]{1,0:T(8,128)S(1)} collective-permute-done((f32[128,512]{1,0:T(8,128)S(1)}, f32[128,512]{1,0:T(8,128)S(1)}, u32[]{:S(2)}, u32[]{:S(2)}) %collective-permute-start.33) | collective-permute-done | bytes 262176 | tf_op jit(solution)/shard_map/ppermute | solution.py:57
  200.8 2.2 collective-permute-done.37.refs_7_
  211.2 18.7 %collective-permute-done.40 = f32[512,512]{1,0:T(8,128)S(1)} collective-permute-done((f32[512,512]{1,0:T(8,128)S(1)}, f32[512,512]{1,0:T(8,128)S(1)}, u32[]{:S(2)}, u32[]{:S(2)}) %collective-permute-start.40) | collective-permute-done | bytes 1048608 | tf_op jit(solution)/shard_map/ppermute | solution.py:57
  231.2 21.1 %collective-permute-done.39 = f32[512,512]{1,0:T(8,128)S(1)} collective-permute-done((f32[512,512]{1,0:T(8,128)S(1)}, f32[512,512]{1,0:T(8,128)S(1)}, u32[]{:S(2)}, u32[]{:S(2)}) %collective-permute-start.39) | collective-permute-done | bytes 1048608 | tf_op jit(solution)/shard_map/ppermute | solution.py:57
  253.9 24.3 %collective-permute-done.42 = f32[512,512]{1,0:T(8,128)S(1)} collective-permute-done((f32[512,512]{1,0:T(8,128)S(1)}, f32[512,512]{1,0:T(8,128)S(1)}, u32[]{:S(2)}, u32[]{:S(2)}) %collective-permute-start.42) | collective-permute-done | bytes 1048608 | tf_op jit(solution)/shard_map/ppermute | solution.py:57
  (82 shorter events, 47.8 us)
Async XLA Ops:
  5.9 11.1 %collective-permute-start.11 = (f32[128,512]{1,0:T(8,128)S(1)}, f32[128,512]{1,0:T(8,128)S(1)}, u32[]{:S(2)}, u32[]{:S(2)}) collective-permute-start(f32[128,512]{1,0:T(8,128)S(1)} %pad_maximum_fusion.2.refs_0_), channel_id=1, source_target_pairs={{0,2},{1,3},{2,4},{3,5},{4,6},{5,7},{6,0},{7,1},{8,10},{9,11},{10,... | collective-permute-start | bytes 786440 | tf_op jit(solution)/shard_map/ppermute | solution.py:57
  7.7 12.4 %collective-permute-start.9 = (f32[128,512]{1,0:T(8,128)S(1)}, f32[128,512]{1,0:T(8,128)S(1)}, u32[]{:S(2)}, u32[]{:S(2)}) collective-permute-start(f32[128,512]{1,0:T(8,128)S(1)} %pad_maximum_fusion.2.refs_0_), channel_id=1, source_target_pairs={{0,6},{1,7},{2,0},{3,1},{4,2},{5,3},{6,4},{7,5},{8,14},{9,15},{10,... | collective-permute-start | bytes 786440 | tf_op jit(solution)/shard_map/ppermute | solution.py:57
  11.0 14.8 %collective-permute-start.13 = (f32[128,512]{1,0:T(8,128)S(1)}, f32[128,512]{1,0:T(8,128)S(1)}, u32[]{:S(2)}, u32[]{:S(2)}) collective-permute-start(f32[128,512]{1,0:T(8,128)S(1)} %collective-permute-done.12.refs_4_), channel_id=1, source_target_pairs={{0,6},{1,7},{2,0},{3,1},{4,2},{5,3},{6,4},{7,5},{8,14},{9,15},{10,... | collective-permute-start | bytes 786440 | tf_op jit(solution)/shard_map/ppermute | solution.py:57
  13.6 12.2 %collective-permute-start.14 = (f32[128,512]{1,0:T(8,128)S(1)}, f32[128,512]{1,0:T(8,128)S(1)}, u32[]{:S(2)}, u32[]{:S(2)}) collective-permute-start(f32[128,512]{1,0:T(8,128)S(1)} %collective-permute-done.10.refs_2_), channel_id=1, source_target_pairs={{0,8},{1,9},{2,10},{3,11},{4,12},{5,13},{6,14},{7,15},{8,0},{9,1},... | collective-permute-start | bytes 786440 | tf_op jit(solution)/shard_map/ppermute | solution.py:57
  13.9 11.9 %collective-permute-start.15 = (f32[128,512]{1,0:T(8,128)S(1)}, f32[128,512]{1,0:T(8,128)S(1)}, u32[]{:S(2)}, u32[]{:S(2)}) collective-permute-start(f32[128,512]{1,0:T(8,128)S(1)} %collective-permute-done.12.refs_4_), channel_id=1, source_target_pairs={{0,2},{1,3},{2,4},{3,5},{4,6},{5,7},{6,0},{7,1},{8,10},{9,11},{10,... | collective-permute-start | bytes 786440 | tf_op jit(solution)/shard_map/ppermute | solution.py:57
  34.2 59.8 %collective-permute-start.25 = (f32[1024,512]{1,0:T(8,128)S(1)}, f32[1024,512]{1,0:T(8,128)S(1)}, u32[]{:S(2)}, u32[]{:S(2)}) collective-permute-start(f32[1024,512]{1,0:T(8,128)S(1)} %fusion.17), channel_id=1, source_target_pairs={{0,1},{1,0},{2,3},{3,2},{4,5},{5,4},{6,7},{7,6},{8,9},{9,8},{10,11... | collective-permute-start | bytes 6291464 | tf_op jit(solution)/shard_map/ppermute | solution.py:57
  34.6 24.2 %collective-permute-start.17 = (f32[128,512]{1,0:T(8,128)S(1)}, f32[128,512]{1,0:T(8,128)S(1)}, u32[]{:S(2)}, u32[]{:S(2)}) collective-permute-start(f32[128,512]{1,0:T(8,128)S(1)} %pad_maximum_fusion.2.refs_0_), channel_id=1, source_target_pairs={{0,0},{1,1},{2,16},{3,17},{4,32},{5,33},{6,48},{7,49},{8,64},{9,65... | collective-permute-start | bytes 786440 | tf_op jit(solution)/shard_map/ppermute | solution.py:57
  39.3 19.5 %collective-permute-start.4 = (f32[128,512]{1,0:T(8,128)S(1)}, f32[128,512]{1,0:T(8,128)S(1)}, u32[]{:S(2)}, u32[]{:S(2)}) collective-permute-start(f32[128,512]{1,0:T(8,128)S(1)} %pad_maximum_fusion.1.refs_0_), channel_id=1, source_target_pairs={{0,8},{1,9},{2,10},{3,11},{4,12},{5,13},{6,14},{7,15},{8,0},{9,1},... | collective-permute-start | bytes 786440 | tf_op jit(solution)/shard_map/ppermute | solution.py:57
  42.1 20.9 %collective-permute-start.2 = (f32[128,512]{1,0:T(8,128)S(1)}, f32[128,512]{1,0:T(8,128)S(1)}, u32[]{:S(2)}, u32[]{:S(2)}) collective-permute-start(f32[128,512]{1,0:T(8,128)S(1)} %pad_maximum_fusion.1.refs_0_), channel_id=1, source_target_pairs={{0,4},{1,5},{2,6},{3,7},{4,0},{5,1},{6,2},{7,3},{8,12},{9,13},{10,... | collective-permute-start | bytes 786440 | tf_op jit(solution)/shard_map/ppermute | solution.py:57
  42.1 20.9 %collective-permute-start.1 = (f32[128,512]{1,0:T(8,128)S(1)}, f32[128,512]{1,0:T(8,128)S(1)}, u32[]{:S(2)}, u32[]{:S(2)}) collective-permute-start(f32[128,512]{1,0:T(8,128)S(1)} %pad_maximum_fusion.1.refs_0_), channel_id=1, source_target_pairs={{0,6},{1,7},{2,0},{3,1},{4,2},{5,3},{6,4},{7,5},{8,14},{9,15},{10,... | collective-permute-start | bytes 786440 | tf_op jit(solution)/shard_map/ppermute | solution.py:57
  58.8 9.3 %collective-permute-start.21 = (f32[128,512]{1,0:T(8,128)S(1)}, f32[128,512]{1,0:T(8,128)S(1)}, u32[]{:S(2)}, u32[]{:S(2)}) collective-permute-start(f32[128,512]{1,0:T(8,128)S(1)} %collective-permute-done.17.refs_0_), channel_id=1, source_target_pairs={{0,64},{1,65},{2,66},{3,67},{4,68},{5,69},{6,70},{7,71},{8,72},{9,... | collective-permute-start | bytes 786440 | tf_op jit(solution)/shard_map/ppermute | solution.py:57
  63.0 14.6 %collective-permute-start.18 = (f32[128,512]{1,0:T(8,128)S(1)}, f32[128,512]{1,0:T(8,128)S(1)}, u32[]{:S(2)}, u32[]{:S(2)}) collective-permute-start(f32[128,512]{1,0:T(8,128)S(1)} %collective-permute-done.17.refs_0_), channel_id=1, source_target_pairs={{0,48},{1,49},{2,50},{3,51},{4,52},{5,53},{6,54},{7,55},{8,56},{9,... | collective-permute-start | bytes 786440 | tf_op jit(solution)/shard_map/ppermute | solution.py:57
  66.2 12.9 %collective-permute-start.5 = (f32[128,512]{1,0:T(8,128)S(1)}, f32[128,512]{1,0:T(8,128)S(1)}, u32[]{:S(2)}, u32[]{:S(2)}) collective-permute-start(f32[128,512]{1,0:T(8,128)S(1)} %collective-permute-done.4.refs_4_), channel_id=1, source_target_pairs={{0,6},{1,7},{2,0},{3,1},{4,2},{5,3},{6,4},{7,5},{8,14},{9,15},{10,... | collective-permute-start | bytes 786440 | tf_op jit(solution)/shard_map/ppermute | solution.py:57
  68.1 12.9 %collective-permute-start.6 = (f32[128,512]{1,0:T(8,128)S(1)}, f32[128,512]{1,0:T(8,128)S(1)}, u32[]{:S(2)}, u32[]{:S(2)}) collective-permute-start(f32[128,512]{1,0:T(8,128)S(1)} %collective-permute-done.2.refs_2_), channel_id=1, source_target_pairs={{0,8},{1,9},{2,10},{3,11},{4,12},{5,13},{6,14},{7,15},{8,0},{9,1},... | collective-permute-start | bytes 786440 | tf_op jit(solution)/shard_map/ppermute | solution.py:57
  70.5 10.7 %collective-permute-start.7 = (f32[128,512]{1,0:T(8,128)S(1)}, f32[128,512]{1,0:T(8,128)S(1)}, u32[]{:S(2)}, u32[]{:S(2)}) collective-permute-start(f32[128,512]{1,0:T(8,128)S(1)} %collective-permute-done.4.refs_4_), channel_id=1, source_target_pairs={{0,2},{1,3},{2,4},{3,5},{4,6},{5,7},{6,0},{7,1},{8,10},{9,11},{10,... | collective-permute-start | bytes 786440 | tf_op jit(solution)/shard_map/ppermute | solution.py:57
  79.0 10.9 %collective-permute-start.22 = (f32[128,512]{1,0:T(8,128)S(1)}, f32[128,512]{1,0:T(8,128)S(1)}, u32[]{:S(2)}, u32[]{:S(2)}) collective-permute-start(f32[128,512]{1,0:T(8,128)S(1)} %collective-permute-done.21.refs_4_), channel_id=1, source_target_pairs={{0,48},{1,49},{2,50},{3,51},{4,52},{5,53},{6,54},{7,55},{8,56},{9,... | collective-permute-start | bytes 786440 | tf_op jit(solution)/shard_map/ppermute | solution.py:57
  81.0 9.0 %collective-permute-start.23 = (f32[128,512]{1,0:T(8,128)S(1)}, f32[128,512]{1,0:T(8,128)S(1)}, u32[]{:S(2)}, u32[]{:S(2)}) collective-permute-start(f32[128,512]{1,0:T(8,128)S(1)} %collective-permute-done.19.refs_2_), channel_id=1, source_target_pairs={{0,64},{1,65},{2,66},{3,67},{4,68},{5,69},{6,70},{7,71},{8,72},{9,... | collective-permute-start | bytes 786440 | tf_op jit(solution)/shard_map/ppermute | solution.py:57
  81.2 10.6 %collective-permute-start.24 = (f32[128,512]{1,0:T(8,128)S(1)}, f32[128,512]{1,0:T(8,128)S(1)}, u32[]{:S(2)}, u32[]{:S(2)}) collective-permute-start(f32[128,512]{1,0:T(8,128)S(1)} %collective-permute-done.21.refs_4_), channel_id=1, source_target_pairs={{0,16},{1,17},{2,18},{3,19},{4,20},{5,21},{6,22},{7,23},{8,24},{9,... | collective-permute-start | bytes 786440 | tf_op jit(solution)/shard_map/ppermute | solution.py:57
  86.1 48.6 %collective-permute-start.8 = (f32[1024,512]{1,0:T(8,128)}, f32[1024,512]{1,0:T(8,128)}, u32[]{:S(2)}, u32[]{:S(2)}) collective-permute-start(f32[1024,512]{1,0:T(8,128)} %shard_map.28.own), channel_id=1, source_target_pairs={{0,1},{1,0},{2,3},{3,2},{4,5},{5,4},{6,7},{7,6},{8,9},{9,8},{10,11... | collective-permute-start | bytes 6291464 | tf_op jit(solution)/shard_map/ppermute | solution.py:57
  95.0 17.7 %collective-permute-start.27 = (f32[512,512]{1,0:T(8,128)S(1)}, f32[512,512]{1,0:T(8,128)S(1)}, u32[]{:S(2)}, u32[]{:S(2)}) collective-permute-start(f32[512,512]{1,0:T(8,128)S(1)} %convolution_add_fusion.2), channel_id=1, source_target_pairs={{0,0},{1,2},{2,4},{3,1},{4,6},{5,3},{6,8},{7,5},{8,10},{9,7},{10,1... | collective-permute-start | bytes 3145736 | tf_op jit(solution)/shard_map/ppermute | solution.py:57
  97.9 35.5 %collective-permute-start.26 = (f32[512,512]{1,0:T(8,128)S(1)}, f32[512,512]{1,0:T(8,128)}, u32[]{:S(2)}, u32[]{:S(2)}) collective-permute-start(f32[512,512]{1,0:T(8,128)S(1)} %convolution_add_fusion.3), channel_id=1, source_target_pairs={{0,0},{1,2},{2,4},{3,1},{4,6},{5,3},{6,8},{7,5},{8,10},{9,7},{10,1... | collective-permute-start | bytes 3145736 | tf_op jit(solution)/shard_map/ppermute | solution.py:57
  112.6 24.6 %collective-permute-start.28 = (f32[512,512]{1,0:T(8,128)S(1)}, f32[512,512]{1,0:T(8,128)}, u32[]{:S(2)}, u32[]{:S(2)}) collective-permute-start(f32[512,512]{1,0:T(8,128)S(1)} %collective-permute-done.27), channel_id=1, source_target_pairs={{0,16},{1,17},{2,18},{3,19},{4,20},{5,21},{6,22},{7,23},{8,24},{9,... | collective-permute-start | bytes 3145736 | tf_op jit(solution)/shard_map/ppermute | solution.py:57
  133.5 21.1 %collective-permute-start.29 = (f32[512,512]{1,0:T(8,128)}, f32[512,512]{1,0:T(8,128)}, u32[]{:S(2)}, u32[]{:S(2)}) collective-permute-start(f32[512,512]{1,0:T(8,128)} %collective-permute-done.26), channel_id=1, source_target_pairs={{16,0},{17,1},{18,2},{19,3},{20,4},{21,5},{22,6},{23,7},{24,8},{25... | collective-permute-start | bytes 3145736 | tf_op jit(solution)/shard_map/ppermute | solution.py:57
  159.5 45.8 %collective-permute-start.38 = (f32[1024,512]{1,0:T(8,128)S(1)}, f32[1024,512]{1,0:T(8,128)S(1)}, u32[]{:S(2)}, u32[]{:S(2)}) collective-permute-start(f32[1024,512]{1,0:T(8,128)S(1)} %fusion), channel_id=1, source_target_pairs={{0,1},{1,0},{2,3},{3,2},{4,5},{5,4},{6,7},{7,6},{8,9},{9,8},{10,11... | collective-permute-start | bytes 6291464 | tf_op jit(solution)/shard_map/ppermute | solution.py:57
  166.3 18.4 %collective-permute-start.30 = (f32[128,512]{1,0:T(8,128)S(1)}, f32[128,512]{1,0:T(8,128)S(1)}, u32[]{:S(2)}, u32[]{:S(2)}) collective-permute-start(f32[128,512]{1,0:T(8,128)S(1)} %pad_maximum_fusion.1.refs_0_), channel_id=1, source_target_pairs={{0,0},{1,1},{2,16},{3,17},{4,32},{5,33},{6,48},{7,49},{8,64},{9,65... | collective-permute-start | bytes 786440 | tf_op jit(solution)/shard_map/ppermute | solution.py:57
  184.7 9.0 %collective-permute-start.32 = (f32[128,512]{1,0:T(8,128)S(1)}, f32[128,512]{1,0:T(8,128)S(1)}, u32[]{:S(2)}, u32[]{:S(2)}) collective-permute-start(f32[128,512]{1,0:T(8,128)S(1)} %collective-permute-done.30.refs_0_), channel_id=1, source_target_pairs={{0,32},{1,33},{2,34},{3,35},{4,36},{5,37},{6,38},{7,39},{8,40},{9,... | collective-permute-start | bytes 786440 | tf_op jit(solution)/shard_map/ppermute | solution.py:57
  184.7 11.7 %collective-permute-start.31 = (f32[128,512]{1,0:T(8,128)S(1)}, f32[128,512]{1,0:T(8,128)S(1)}, u32[]{:S(2)}, u32[]{:S(2)}) collective-permute-start(f32[128,512]{1,0:T(8,128)S(1)} %collective-permute-done.30.refs_0_), channel_id=1, source_target_pairs={{0,48},{1,49},{2,50},{3,51},{4,52},{5,53},{6,54},{7,55},{8,56},{9,... | collective-permute-start | bytes 786440 | tf_op jit(solution)/shard_map/ppermute | solution.py:57
  184.7 15.3 %collective-permute-start.33 = (f32[128,512]{1,0:T(8,128)S(1)}, f32[128,512]{1,0:T(8,128)S(1)}, u32[]{:S(2)}, u32[]{:S(2)}) collective-permute-start(f32[128,512]{1,0:T(8,128)S(1)} %collective-permute-done.30.refs_0_), channel_id=1, source_target_pairs={{0,16},{1,17},{2,18},{3,19},{4,20},{5,21},{6,22},{7,23},{8,24},{9,... | collective-permute-start | bytes 786440 | tf_op jit(solution)/shard_map/ppermute | solution.py:57
  206.3 23.6 %collective-permute-start.40 = (f32[512,512]{1,0:T(8,128)S(1)}, f32[512,512]{1,0:T(8,128)S(1)}, u32[]{:S(2)}, u32[]{:S(2)}) collective-permute-start(f32[512,512]{1,0:T(8,128)S(1)} %convolution_add_fusion), channel_id=1, source_target_pairs={{0,0},{1,2},{2,4},{3,1},{4,6},{5,3},{6,8},{7,5},{8,10},{9,7},{10,1... | collective-permute-start | bytes 3145736 | tf_op jit(solution)/shard_map/ppermute | solution.py:57
  209.2 43.1 %collective-permute-start.39 = (f32[512,512]{1,0:T(8,128)S(1)}, f32[512,512]{1,0:T(8,128)S(1)}, u32[]{:S(2)}, u32[]{:S(2)}) collective-permute-start(f32[512,512]{1,0:T(8,128)S(1)} %convolution_add_fusion.1), channel_id=1, source_target_pairs={{0,0},{1,2},{2,4},{3,1},{4,6},{5,3},{6,8},{7,5},{8,10},{9,7},{10,1... | collective-permute-start | bytes 3145736 | tf_op jit(solution)/shard_map/ppermute | solution.py:57
  229.9 23.8 %collective-permute-start.41 = (f32[512,512]{1,0:T(8,128)S(1)}, f32[512,512]{1,0:T(8,128)S(1)}, u32[]{:S(2)}, u32[]{:S(2)}) collective-permute-start(f32[512,512]{1,0:T(8,128)S(1)} %collective-permute-done.40), channel_id=1, source_target_pairs={{0,16},{1,17},{2,18},{3,19},{4,20},{5,21},{6,22},{7,23},{8,24},{9,... | collective-permute-start | bytes 3145736 | tf_op jit(solution)/shard_map/ppermute | solution.py:57
  252.3 25.8 %collective-permute-start.42 = (f32[512,512]{1,0:T(8,128)S(1)}, f32[512,512]{1,0:T(8,128)S(1)}, u32[]{:S(2)}, u32[]{:S(2)}) collective-permute-start(f32[512,512]{1,0:T(8,128)S(1)} %collective-permute-done.39), channel_id=1, source_target_pairs={{16,0},{17,1},{18,2},{19,3},{20,4},{21,5},{22,6},{23,7},{24,8},{25... | collective-permute-start | bytes 3145736 | tf_op jit(solution)/shard_map/ppermute | solution.py:57
  (12 other events, 106.4 us)
where the time goes:
time: 280 us
  waiting for transfers between devices  194 us (69%)
  starting transfers between devices  59 us (21%)
  matrix products  15.2 us (5%)
  other arithmetic  4.82 us (2%)
  Pallas kernels  4.7 us (2%)
    ppermute x43, waiting for transfers between devices, send(): return lax.ppermute(value, ('row', 'col'), pairs)  194 us
    ppermute x43, starting transfers between devices, send(): return lax.ppermute(value, ('row', 'col'), pairs)  59 us
    dot_general x8, matrix products, times(): return jnp.dot(tile, turn, precision=HIGH, preferred_element_type=F32)  8.1 us
    dot_general x2, matrix products, mix(): lax.dot_general(turn, tile, dims, precision=HIGH, preferred_element_type=...  7.07 us
  transfers between devices with their start and end apart: 43, of which 25 were waited for; matrix products, arithmetic and copies ran while one was open for 3% of the time, Pallas kernels for 2%

commit v1 on v0

--- a/solution.py
+++ b/solution.py
@@ -48,9 +48,25 @@
     return old + 2 if old % 2 == 0 else old - 2
 
 
-MOVE_COL = [(r * 16 + c, r * 16 + new_position(c)) for r in range(8) for c in range(16)]
-ROW_UP = [(r * 16 + c, (r + 1) * 16 + c) for r in range(7) for c in range(16)]
-ROW_DOWN = [(r * 16 + c, (r - 1) * 16 + c) for r in range(1, 8) for c in range(16)]
+RELAYED = {(3, 0): (4, 8), (4, 0): (3, 8), (3, 14): (4, 6), (4, 14): (3, 6)}
+
+
+def moves(rises):
+    out = []
+    for r in range(8):
+        for c in range(16):
+            to = r + 1 if rises(c) else r - 1
+            relayed = (r, c) in RELAYED and {r, to} == {3, 4}
+            if 0 <= to < 8 and not relayed:
+                out.append((r * 16 + c, to * 16 + new_position(c)))
+    return out
+
+
+MOVE_FIRST = moves(lambda c: c % 2 == 0)
+MOVE_SECOND = moves(lambda c: c % 2 == 1)
+MOVE_END = [(r * 16 + c, r * 16 + new_position(c)) for r in (0, 7) for c in range(16)]
+MOVE_END += [(r * 16 + c, to[0] * 16 + to[1]) for (r, c), to in RELAYED.items()]
+FROM_RELAY = [(to[0] * 16 + to[1], to[0] * 16 + new_position(c)) for (_, c), to in RELAYED.items()]
 
 
 def send(value, pairs):
@@ -81,14 +97,14 @@
 
 
 def join_body(own, other, out):
-    up_is_own = (lax.axis_index("col") % 2 == 0) != (lax.axis_index("row") == 0)
-
-    @pl.when(up_is_own)
+    own_first = lax.axis_index("row") != 0
+
+    @pl.when(own_first)
     def _():
         out[:, 0:N] = own[...]
         out[:, N:] = other[...]
 
-    @pl.when(jnp.logical_not(up_is_own))
+    @pl.when(jnp.logical_not(own_first))
     def _():
         out[:, 0:N] = other[...]
         out[:, N:] = own[...]
@@ -143,8 +159,10 @@
 
 
 def shards(gram, rotations):
-    row = lax.axis_index("row")
-    core = lax.axis_index("col") % 2
+    row, col = lax.axis_index("row"), lax.axis_index("col")
+    core = col % 2
+    from_even = ((core == 0) & (col != 2)) | (col == 15)
+    by_relay = (col == 0) | (col == 15)
     keep = lax.dynamic_slice_in_dim(rotations[:, 0], core * N, N, 2)
     give = lax.dynamic_slice_in_dim(rotations[:, 0], (1 - core) * N, N, 2)
     got = send(give, OTHER_CORE)
@@ -164,16 +182,21 @@
         mixed = mix(rows, tile)
         other = send(mixed, OTHER_CORE)
         own_parts = times(mixed[:N], own_cols), times(mixed[N:], own_cols)
-        up, down = lax.optimization_barrier(own_parts)
-        up = up + times(other[:N], other_cols)
-        down = down + times(other[N:], other_cols)
-        up = send(up, MOVE_COL)
-        down = send(down, MOVE_COL)
-        from_above = send(up, ROW_UP)
-        from_below = send(down, ROW_DOWN)
-        first = jnp.where(row == 0, down, from_above)
-        second = jnp.where(row == 7, up, from_below)
-        return jnp.concatenate([first, second])
+        first, second = lax.optimization_barrier(own_parts)
+        first = first + times(other[N:], other_cols)
+        second = second + times(other[:N], other_cols)
+        first, second = lax.optimization_barrier((first, second))
+        end_is_first = ((row == 7) == (core == 0)) & (row != 4)
+        ends = jnp.where((row == 3) | end_is_first, first, second)
+        first = send(first, MOVE_FIRST)
+        ends = send(ends, MOVE_END)
+        second = send(second, MOVE_SECOND)
+        relayed = send(ends, FROM_RELAY)
+        first = jnp.where(by_relay & (row == 4), relayed, first)
+        second = jnp.where(by_relay & (row == 3), relayed, second)
+        upper = jnp.where(row == 0, ends, jnp.where(from_even, first, second))
+        lower = jnp.where(row == 7, ends, jnp.where(from_even, second, first))
+        return jnp.concatenate([upper, lower])
 
     tile = gram
     for step in ("1", "2"):

time: 280 us -> 273 us (0.975)
  the two profiles are of different devices: /device:TPU:7 before, /device:TPU:24 now
where the time goes in v1:
time: 273 us; the launch traced here: 272 us
  waiting for transfers between devices  159 us (58%)
  starting transfers between devices  70.1 us (26%)
  matrix products  22.4 us (8%)
  local copies, waits for them, and re-layouts  7.82 us (3%)
  Pallas kernels  6.12 us (2%)
  other arithmetic  6.04 us (2%)
    ppermute x43, waiting for transfers between devices, send(): return lax.ppermute(value, ('row', 'col'), pairs)  159 us
    ppermute x43, starting transfers between devices, send(): return lax.ppermute(value, ('row', 'col'), pairs)  70.1 us
    dot_general x8, matrix products, times(): return jnp.dot(tile, turn, precision=HIGH, preferred_element_type=F32)  14 us
    dot_general x2, matrix products, mix(): lax.dot_general(turn, tile, dims, precision=HIGH, preferred_element_type=...  8.44 us
    pallas_call x6, Pallas kernels, vmem_call(): pl.pallas_call(body, out_shape=[jax.ShapeDtypeStruct(shape, F32) for shap...  6.12 us
    unnamed x18, local copies, waits for them, and re-layouts  5.69 us
  transfers between devices with their start and end apart: 43, of which 26 were waited for; matrix products, arithmetic and copies ran while one was open for 5% of the time, Pallas kernels for 2%

profile of v1, /device:TPU:24, one launch (start us, length us, event | category | flops | bytes accessed | tf_op | source)
XLA Modules:
  0.0 271.6 jit_solution(6620299636859172002)
XLA Ops:
  4.8 3.0 %collective-permute-start.10 = (f32[128,512]{1,0:T(8,128)S(1)}, f32[128,512]{1,0:T(8,128)S(1)}, u32[]{:S(2)}, u32[]{:S(2)}) collective-permute-start(f32[128,512]{1,0:T(8,128)S(1)} %pad_maximum_fusion.2.refs_0_), channel_id=1, source_target_pairs={{0,4},{1,5},{2,6},{3,7},{4,0},{5,1},{6,2},{7,3},{8,12},{9,13},{10,... | collective-permute-start | bytes 786440 | tf_op jit(solution)/shard_map/ppermute | solution.py:73
  8.4 2.6 collective-permute-start.9
  11.4 2.8 %collective-permute-start.13 = (f32[128,512]{1,0:T(8,128)S(1)}, f32[128,512]{1,0:T(8,128)S(1)}, u32[]{:S(2)}, u32[]{:S(2)}) collective-permute-start(f32[128,512]{1,0:T(8,128)S(1)} %collective-permute-done.12.refs_4_), channel_id=1, source_target_pairs={{0,6},{1,7},{2,0},{3,1},{4,2},{5,3},{6,4},{7,5},{8,14},{9,15},{10,... | collective-permute-start | bytes 786440 | tf_op jit(solution)/shard_map/ppermute | solution.py:73
  17.1 3.0 %collective-permute-done.11.refs_3_ = f32[128,512]{1,0:T(8,128)S(1)} collective-permute-done((f32[128,512]{1,0:T(8,128)S(1)}, f32[128,512]{1,0:T(8,128)S(1)}, u32[]{:S(2)}, u32[]{:S(2)}) %collective-permute-start.11) | collective-permute-done | bytes 262176 | tf_op jit(solution)/shard_map/ppermute | solution.py:73
  21.2 4.5 %collective-permute-done.13.refs_5_ = f32[128,512]{1,0:T(8,128)S(1)} collective-permute-done((f32[128,512]{1,0:T(8,128)S(1)}, f32[128,512]{1,0:T(8,128)S(1)}, u32[]{:S(2)}, u32[]{:S(2)}) %collective-permute-start.13) | collective-permute-done | bytes 262176 | tf_op jit(solution)/shard_map/ppermute | solution.py:73
  26.0 4.1 %collective-permute-done.16.other = f32[1024,512]{1,0:T(8,128)S(1)} collective-permute-done((f32[1024,512]{1,0:T(8,128)S(1)}, f32[1024,512]{1,0:T(8,128)S(1)}, u32[]{:S(2)}, u32[]{:S(2)}) %collective-permute-start.16) | collective-permute-done | bytes 2097184 | tf_op jit(solution)/shard_map/ppermute | solution.py:73
  30.4 4.9 %fusion.17 = f32[1024,512]{1,0:T(8,128)} fusion(f32[1024,1024]{1,0:T(8,128)S(1)} %shard_map.31, f32[1024,512]{1,0:T(8,128)S(1)} %copy-done), kind=kOutput, calls=%fused_computation.39 | convolution fusion | flops 3221225472 | bytes 8388608 | tf_op jit(solution)/shard_map/dot_general | solution.py:137
  35.5 4.2 %collective-permute-start.17 = (f32[128,512]{1,0:T(8,128)S(1)}, f32[128,512]{1,0:T(8,128)}, u32[]{:S(2)}, u32[]{:S(2)}) collective-permute-start(f32[128,512]{1,0:T(8,128)S(1)} %pad_maximum_fusion.2.refs_0_), channel_id=1, source_target_pairs={{0,0},{1,1},{2,16},{3,17},{4,32},{5,33},{6,48},{7,49},{8,64},{9,65... | collective-permute-start | bytes 786440 | tf_op jit(solution)/shard_map/ppermute | solution.py:73
  39.7 3.1 %collective-permute-start.4 = (f32[128,512]{1,0:T(8,128)S(1)}, f32[128,512]{1,0:T(8,128)S(1)}, u32[]{:S(2)}, u32[]{:S(2)}) collective-permute-start(f32[128,512]{1,0:T(8,128)S(1)} %pad_maximum_fusion.1.refs_0_), channel_id=1, source_target_pairs={{0,8},{1,9},{2,10},{3,11},{4,12},{5,13},{6,14},{7,15},{8,0},{9,1},... | collective-permute-start | bytes 786440 | tf_op jit(solution)/shard_map/ppermute | solution.py:73
  44.8 2.6 collective-permute-start.1
  47.3 13.3 %collective-permute-done.17.refs_0_ = f32[128,512]{1,0:T(8,128)} collective-permute-done((f32[128,512]{1,0:T(8,128)S(1)}, f32[128,512]{1,0:T(8,128)}, u32[]{:S(2)}, u32[]{:S(2)}) %collective-permute-start.17) | collective-permute-done | bytes 262176 | tf_op jit(solution)/shard_map/ppermute | solution.py:73
  60.6 4.5 %collective-permute-start.21 = (f32[128,512]{1,0:T(8,128)}, f32[128,512]{1,0:T(8,128)}, u32[]{:S(2)}, u32[]{:S(2)}) collective-permute-start(f32[128,512]{1,0:T(8,128)} %collective-permute-done.17.refs_0_), channel_id=1, source_target_pairs={{0,64},{1,65},{2,66},{3,67},{4,68},{5,69},{6,70},{7,71},{8,72},{9,... | collective-permute-start | bytes 786440 | tf_op jit(solution)/shard_map/ppermute | solution.py:73
  65.5 4.0 %collective-permute-done.3.refs_3_ = f32[128,512]{1,0:T(8,128)S(1)} collective-permute-done((f32[128,512]{1,0:T(8,128)S(1)}, f32[128,512]{1,0:T(8,128)S(1)}, u32[]{:S(2)}, u32[]{:S(2)}) %collective-permute-start.3) | collective-permute-done | bytes 262176 | tf_op jit(solution)/shard_map/ppermute | solution.py:73
  71.5 4.6 %collective-permute-done.19.refs_2_ = f32[128,512]{1,0:T(8,128)} collective-permute-done((f32[128,512]{1,0:T(8,128)}, f32[128,512]{1,0:T(8,128)}, u32[]{:S(2)}, u32[]{:S(2)}) %collective-permute-start.19) | collective-permute-done | bytes 262176 | tf_op jit(solution)/shard_map/ppermute | solution.py:73
  76.1 3.6 %collective-permute-done.18.refs_1_ = f32[128,512]{1,0:T(8,128)S(1)} collective-permute-done((f32[128,512]{1,0:T(8,128)}, f32[128,512]{1,0:T(8,128)S(1)}, u32[]{:S(2)}, u32[]{:S(2)}) %collective-permute-start.18) | collective-permute-done | bytes 262176 | tf_op jit(solution)/shard_map/ppermute | solution.py:73
  102.7 3.2 %convolution_add_fusion.3 = f32[512,512]{1,0:T(8,128)} fusion(f32[512,512]{1,0:T(8,128)S(1)} %fusion.14, f32[512,512]{1,0:T(8,128)S(1)} %get-tuple-element.19, f32[1024,512]{1,0:T(8,128)} %collective-permute-done.25), kind=kOutput, calls=%fused_computation.8 | convolution fusion | flops 805568512 | bytes 4194304 | tf_op jit(solution)/shard_map/dot_general | solution.py:141
  107.4 3.5 %collective-permute-start.26 = (f32[512,512]{1,0:T(8,128)S(1)}, f32[512,512]{1,0:T(8,128)}, u32[]{:S(2)}, u32[]{:S(2)}) collective-permute-start(f32[512,512]{1,0:T(8,128)S(1)} %broadcast_select_fusion.5), channel_id=1, source_target_pairs={{0,0},{1,2},{2,4},{3,1},{4,6},{5,3},{6,8},{7,5},{8,10},{9,7},{10,1... | collective-permute-start | bytes 3145736 | tf_op jit(solution)/shard_map/ppermute | solution.py:73
  112.1 5.5 %collective-permute-start.29 = (f32[512,512]{1,0:T(8,128)S(1)}, f32[512,512]{1,0:T(8,128)}, u32[]{:S(2)}, u32[]{:S(2)}) collective-permute-start(f32[512,512]{1,0:T(8,128)S(1)} %convolution_add_fusion.2), channel_id=1, source_target_pairs={{1,18},{3,17},{5,19},{7,21},{9,23},{11,25},{13,27},{15,29},{16,0},... | collective-permute-start | bytes 3145736 | tf_op jit(solution)/shard_map/ppermute | solution.py:73
  117.7 27.0 %collective-permute-done.26 = f32[512,512]{1,0:T(8,128)} collective-permute-done((f32[512,512]{1,0:T(8,128)S(1)}, f32[512,512]{1,0:T(8,128)}, u32[]{:S(2)}, u32[]{:S(2)}) %collective-permute-start.26) | collective-permute-done | bytes 1048608 | tf_op jit(solution)/shard_map/ppermute | solution.py:73
  146.0 2.5 shard_map.29
  149.0 15.1 %collective-permute-done.27 = f32[512,512]{1,0:T(8,128)} collective-permute-done((f32[512,512]{1,0:T(8,128)}, f32[512,512]{1,0:T(8,128)}, u32[]{:S(2)}, u32[]{:S(2)}) %collective-permute-start.27) | collective-permute-done | bytes 1048608 | tf_op jit(solution)/shard_map/ppermute | solution.py:73
  164.1 2.4 select_select_fusion.3
  166.5 3.5 %fusion = f32[1024,512]{1,0:T(8,128)S(1)} fusion(f32[1024,1024]{1,0:T(8,128)S(1)} %shard_map.29, f32[512,512]{1,0:T(8,128)S(1)} %get-tuple-element.32, f32[512,512]{1,0:T(8,128)S(1)} %get-tuple-element.31), kind=kOutput, calls=%fused_computation | convolution fusion | flops 3221749760 | bytes 8388608 | tf_op jit(solution)/shard_map/dot_general | solution.py:137
  172.0 12.0 %collective-permute-done.30.refs_0_ = f32[128,512]{1,0:T(8,128)S(1)} collective-permute-done((f32[128,512]{1,0:T(8,128)S(1)}, f32[128,512]{1,0:T(8,128)S(1)}, u32[]{:S(2)}, u32[]{:S(2)}) %collective-permute-start.30) | collective-permute-done | bytes 262176 | tf_op jit(solution)/shard_map/ppermute | solution.py:73
  184.4 2.9 %collective-permute-start.33 = (f32[128,512]{1,0:T(8,128)S(1)}, f32[128,512]{1,0:T(8,128)S(1)}, u32[]{:S(2)}, u32[]{:S(2)}) collective-permute-start(f32[128,512]{1,0:T(8,128)S(1)} %collective-permute-done.30.refs_0_), channel_id=1, source_target_pairs={{0,16},{1,17},{2,18},{3,19},{4,20},{5,21},{6,22},{7,23},{8,24},{9,... | collective-permute-start | bytes 786440 | tf_op jit(solution)/shard_map/ppermute | solution.py:73
  187.3 6.1 %collective-permute-done.34.refs_4_ = f32[128,512]{1,0:T(8,128)S(1)} collective-permute-done((f32[128,512]{1,0:T(8,128)S(1)}, f32[128,512]{1,0:T(8,128)S(1)}, u32[]{:S(2)}, u32[]{:S(2)}) %collective-permute-start.34) | collective-permute-done | bytes 262176 | tf_op jit(solution)/shard_map/ppermute | solution.py:73
  194.7 3.5 %collective-permute-start.36 = (f32[128,512]{1,0:T(8,128)S(1)}, f32[128,512]{1,0:T(8,128)S(1)}, u32[]{:S(2)}, u32[]{:S(2)}) collective-permute-start(f32[128,512]{1,0:T(8,128)S(1)} %collective-permute-done.32.refs_2_), channel_id=1, source_target_pairs={{0,64},{1,65},{2,66},{3,67},{4,68},{5,69},{6,70},{7,71},{8,72},{9,... | collective-permute-start | bytes 786440 | tf_op jit(solution)/shard_map/ppermute | solution.py:73
  200.9 3.4 %collective-permute-done.35.refs_5_ = f32[128,512]{1,0:T(8,128)S(1)} collective-permute-done((f32[128,512]{1,0:T(8,128)S(1)}, f32[128,512]{1,0:T(8,128)S(1)}, u32[]{:S(2)}, u32[]{:S(2)}) %collective-permute-start.35) | collective-permute-done | bytes 262176 | tf_op jit(solution)/shard_map/ppermute | solution.py:73
  211.1 6.7 %collective-permute-start.39 = (f32[512,512]{1,0:T(8,128)S(1)}, f32[512,512]{1,0:T(8,128)S(1)}, u32[]{:S(2)}, u32[]{:S(2)}) collective-permute-start(f32[512,512]{1,0:T(8,128)S(1)} %broadcast_select_fusion.4), channel_id=1, source_target_pairs={{0,0},{1,2},{2,4},{3,1},{4,6},{5,3},{6,8},{7,5},{8,10},{9,7},{10,1... | collective-permute-start | bytes 3145736 | tf_op jit(solution)/shard_map/ppermute | solution.py:73
  219.1 4.6 %collective-permute-start.42 = (f32[512,512]{1,0:T(8,128)S(1)}, f32[512,512]{1,0:T(8,128)S(1)}, u32[]{:S(2)}, u32[]{:S(2)}) collective-permute-start(f32[512,512]{1,0:T(8,128)S(1)} %convolution_add_fusion), channel_id=1, source_target_pairs={{1,18},{3,17},{5,19},{7,21},{9,23},{11,25},{13,27},{15,29},{16,0},... | collective-permute-start | bytes 3145736 | tf_op jit(solution)/shard_map/ppermute | solution.py:73
  223.7 29.2 %collective-permute-done.39 = f32[512,512]{1,0:T(8,128)S(1)} collective-permute-done((f32[512,512]{1,0:T(8,128)S(1)}, f32[512,512]{1,0:T(8,128)S(1)}, u32[]{:S(2)}, u32[]{:S(2)}) %collective-permute-start.39) | collective-permute-done | bytes 1048608 | tf_op jit(solution)/shard_map/ppermute | solution.py:73
  254.8 14.9 %collective-permute-done.40 = f32[512,512]{1,0:T(8,128)S(1)} collective-permute-done((f32[512,512]{1,0:T(8,128)S(1)}, f32[512,512]{1,0:T(8,128)S(1)}, u32[]{:S(2)}, u32[]{:S(2)}) %collective-permute-start.40) | collective-permute-done | bytes 1048608 | tf_op jit(solution)/shard_map/ppermute | solution.py:73
  (98 shorter events, 60.4 us)
Async XLA Ops:
  4.8 10.7 %collective-permute-start.10 = (f32[128,512]{1,0:T(8,128)S(1)}, f32[128,512]{1,0:T(8,128)S(1)}, u32[]{:S(2)}, u32[]{:S(2)}) collective-permute-start(f32[128,512]{1,0:T(8,128)S(1)} %pad_maximum_fusion.2.refs_0_), channel_id=1, source_target_pairs={{0,4},{1,5},{2,6},{3,7},{4,0},{5,1},{6,2},{7,3},{8,12},{9,13},{10,... | collective-permute-start | bytes 786440 | tf_op jit(solution)/shard_map/ppermute | solution.py:73
  7.8 12.3 %collective-permute-start.11 = (f32[128,512]{1,0:T(8,128)S(1)}, f32[128,512]{1,0:T(8,128)S(1)}, u32[]{:S(2)}, u32[]{:S(2)}) collective-permute-start(f32[128,512]{1,0:T(8,128)S(1)} %pad_maximum_fusion.2.refs_0_), channel_id=1, source_target_pairs={{0,2},{1,3},{2,4},{3,5},{4,6},{5,7},{6,0},{7,1},{8,10},{9,11},{10,... | collective-permute-start | bytes 786440 | tf_op jit(solution)/shard_map/ppermute | solution.py:73
  8.4 12.8 %collective-permute-start.9 = (f32[128,512]{1,0:T(8,128)S(1)}, f32[128,512]{1,0:T(8,128)S(1)}, u32[]{:S(2)}, u32[]{:S(2)}) collective-permute-start(f32[128,512]{1,0:T(8,128)S(1)} %pad_maximum_fusion.2.refs_0_), channel_id=1, source_target_pairs={{0,6},{1,7},{2,0},{3,1},{4,2},{5,3},{6,4},{7,5},{8,14},{9,15},{10,... | collective-permute-start | bytes 786440 | tf_op jit(solution)/shard_map/ppermute | solution.py:73
  11.4 14.3 %collective-permute-start.13 = (f32[128,512]{1,0:T(8,128)S(1)}, f32[128,512]{1,0:T(8,128)S(1)}, u32[]{:S(2)}, u32[]{:S(2)}) collective-permute-start(f32[128,512]{1,0:T(8,128)S(1)} %collective-permute-done.12.refs_4_), channel_id=1, source_target_pairs={{0,6},{1,7},{2,0},{3,1},{4,2},{5,3},{6,4},{7,5},{8,14},{9,15},{10,... | collective-permute-start | bytes 786440 | tf_op jit(solution)/shard_map/ppermute | solution.py:73
  15.5 10.2 %collective-permute-start.14 = (f32[128,512]{1,0:T(8,128)S(1)}, f32[128,512]{1,0:T(8,128)S(1)}, u32[]{:S(2)}, u32[]{:S(2)}) collective-permute-start(f32[128,512]{1,0:T(8,128)S(1)} %collective-permute-done.10.refs_2_), channel_id=1, source_target_pairs={{0,8},{1,9},{2,10},{3,11},{4,12},{5,13},{6,14},{7,15},{8,0},{9,1},... | collective-permute-start | bytes 786440 | tf_op jit(solution)/shard_map/ppermute | solution.py:73
  15.9 9.8 %collective-permute-start.15 = (f32[128,512]{1,0:T(8,128)S(1)}, f32[128,512]{1,0:T(8,128)S(1)}, u32[]{:S(2)}, u32[]{:S(2)}) collective-permute-start(f32[128,512]{1,0:T(8,128)S(1)} %collective-permute-done.12.refs_4_), channel_id=1, source_target_pairs={{0,2},{1,3},{2,4},{3,5},{4,6},{5,7},{6,0},{7,1},{8,10},{9,11},{10,... | collective-permute-start | bytes 786440 | tf_op jit(solution)/shard_map/ppermute | solution.py:73
  35.4 65.1 %collective-permute-start.25 = (f32[1024,512]{1,0:T(8,128)}, f32[1024,512]{1,0:T(8,128)}, u32[]{:S(2)}, u32[]{:S(2)}) collective-permute-start(f32[1024,512]{1,0:T(8,128)} %fusion.17), channel_id=1, source_target_pairs={{0,1},{1,0},{2,3},{3,2},{4,5},{5,4},{6,7},{7,6},{8,9},{9,8},{10,11... | collective-permute-start | bytes 6291464 | tf_op jit(solution)/shard_map/ppermute | solution.py:73
  35.5 25.1 %collective-permute-start.17 = (f32[128,512]{1,0:T(8,128)S(1)}, f32[128,512]{1,0:T(8,128)}, u32[]{:S(2)}, u32[]{:S(2)}) collective-permute-start(f32[128,512]{1,0:T(8,128)S(1)} %pad_maximum_fusion.2.refs_0_), channel_id=1, source_target_pairs={{0,0},{1,1},{2,16},{3,17},{4,32},{5,33},{6,48},{7,49},{8,64},{9,65... | collective-permute-start | bytes 786440 | tf_op jit(solution)/shard_map/ppermute | solution.py:73
  39.7 20.9 %collective-permute-start.4 = (f32[128,512]{1,0:T(8,128)S(1)}, f32[128,512]{1,0:T(8,128)S(1)}, u32[]{:S(2)}, u32[]{:S(2)}) collective-permute-start(f32[128,512]{1,0:T(8,128)S(1)} %pad_maximum_fusion.1.refs_0_), channel_id=1, source_target_pairs={{0,8},{1,9},{2,10},{3,11},{4,12},{5,13},{6,14},{7,15},{8,0},{9,1},... | collective-permute-start | bytes 786440 | tf_op jit(solution)/shard_map/ppermute | solution.py:73
  42.8 22.3 %collective-permute-start.2 = (f32[128,512]{1,0:T(8,128)S(1)}, f32[128,512]{1,0:T(8,128)S(1)}, u32[]{:S(2)}, u32[]{:S(2)}) collective-permute-start(f32[128,512]{1,0:T(8,128)S(1)} %pad_maximum_fusion.1.refs_0_), channel_id=1, source_target_pairs={{0,4},{1,5},{2,6},{3,7},{4,0},{5,1},{6,2},{7,3},{8,12},{9,13},{10,... | collective-permute-start | bytes 786440 | tf_op jit(solution)/shard_map/ppermute | solution.py:73
  44.8 20.4 %collective-permute-start.1 = (f32[128,512]{1,0:T(8,128)S(1)}, f32[128,512]{1,0:T(8,128)S(1)}, u32[]{:S(2)}, u32[]{:S(2)}) collective-permute-start(f32[128,512]{1,0:T(8,128)S(1)} %pad_maximum_fusion.1.refs_0_), channel_id=1, source_target_pairs={{0,6},{1,7},{2,0},{3,1},{4,2},{5,3},{6,4},{7,5},{8,14},{9,15},{10,... | collective-permute-start | bytes 786440 | tf_op jit(solution)/shard_map/ppermute | solution.py:73
  60.6 10.8 %collective-permute-start.21 = (f32[128,512]{1,0:T(8,128)}, f32[128,512]{1,0:T(8,128)}, u32[]{:S(2)}, u32[]{:S(2)}) collective-permute-start(f32[128,512]{1,0:T(8,128)} %collective-permute-done.17.refs_0_), channel_id=1, source_target_pairs={{0,64},{1,65},{2,66},{3,67},{4,68},{5,69},{6,70},{7,71},{8,72},{9,... | collective-permute-start | bytes 786440 | tf_op jit(solution)/shard_map/ppermute | solution.py:73
  65.1 11.0 %collective-permute-start.19 = (f32[128,512]{1,0:T(8,128)}, f32[128,512]{1,0:T(8,128)}, u32[]{:S(2)}, u32[]{:S(2)}) collective-permute-start(f32[128,512]{1,0:T(8,128)} %collective-permute-done.17.refs_0_), channel_id=1, source_target_pairs={{0,32},{1,33},{2,34},{3,35},{4,36},{5,37},{6,38},{7,39},{8,40},{9,... | collective-permute-start | bytes 786440 | tf_op jit(solution)/shard_map/ppermute | solution.py:73
  65.1 14.6 %collective-permute-start.18 = (f32[128,512]{1,0:T(8,128)}, f32[128,512]{1,0:T(8,128)S(1)}, u32[]{:S(2)}, u32[]{:S(2)}) collective-permute-start(f32[128,512]{1,0:T(8,128)} %collective-permute-done.17.refs_0_), channel_id=1, source_target_pairs={{0,48},{1,49},{2,50},{3,51},{4,52},{5,53},{6,54},{7,55},{8,56},{9,... | collective-permute-start | bytes 786440 | tf_op jit(solution)/shard_map/ppermute | solution.py:73
  69.6 11.7 %collective-permute-start.5 = (f32[128,512]{1,0:T(8,128)S(1)}, f32[128,512]{1,0:T(8,128)S(1)}, u32[]{:S(2)}, u32[]{:S(2)}) collective-permute-start(f32[128,512]{1,0:T(8,128)S(1)} %collective-permute-done.4.refs_4_), channel_id=1, source_target_pairs={{0,6},{1,7},{2,0},{3,1},{4,2},{5,3},{6,4},{7,5},{8,14},{9,15},{10,... | collective-permute-start | bytes 786440 | tf_op jit(solution)/shard_map/ppermute | solution.py:73
  71.4 11.7 %collective-permute-start.6 = (f32[128,512]{1,0:T(8,128)S(1)}, f32[128,512]{1,0:T(8,128)S(1)}, u32[]{:S(2)}, u32[]{:S(2)}) collective-permute-start(f32[128,512]{1,0:T(8,128)S(1)} %collective-permute-done.2.refs_2_), channel_id=1, source_target_pairs={{0,8},{1,9},{2,10},{3,11},{4,12},{5,13},{6,14},{7,15},{8,0},{9,1},... | collective-permute-start | bytes 786440 | tf_op jit(solution)/shard_map/ppermute | solution.py:73
  80.4 10.9 %collective-permute-start.20 = (f32[128,512]{1,0:T(8,128)}, f32[128,512]{1,0:T(8,128)}, u32[]{:S(2)}, u32[]{:S(2)}) collective-permute-start(f32[128,512]{1,0:T(8,128)} %collective-permute-done.17.refs_0_), channel_id=1, source_target_pairs={{0,16},{1,17},{2,18},{3,19},{4,20},{5,21},{6,22},{7,23},{8,24},{9,... | collective-permute-start | bytes 786440 | tf_op jit(solution)/shard_map/ppermute | solution.py:73
  91.3 54.7 %collective-permute-start.8 = (f32[1024,512]{1,0:T(8,128)}, f32[1024,512]{1,0:T(8,128)}, u32[]{:S(2)}, u32[]{:S(2)}) collective-permute-start(f32[1024,512]{1,0:T(8,128)} %shard_map.28.own), channel_id=1, source_target_pairs={{0,1},{1,0},{2,3},{3,2},{4,5},{5,4},{6,7},{7,6},{8,9},{9,8},{10,11... | collective-permute-start | bytes 6291464 | tf_op jit(solution)/shard_map/ppermute | solution.py:73
  107.4 37.3 %collective-permute-start.26 = (f32[512,512]{1,0:T(8,128)S(1)}, f32[512,512]{1,0:T(8,128)}, u32[]{:S(2)}, u32[]{:S(2)}) collective-permute-start(f32[512,512]{1,0:T(8,128)S(1)} %broadcast_select_fusion.5), channel_id=1, source_target_pairs={{0,0},{1,2},{2,4},{3,1},{4,6},{5,3},{6,8},{7,5},{8,10},{9,7},{10,1... | collective-permute-start | bytes 3145736 | tf_op jit(solution)/shard_map/ppermute | solution.py:73
  110.9 38.2 %collective-permute-start.28 = (f32[512,512]{1,0:T(8,128)}, f32[512,512]{1,0:T(8,128)}, u32[]{:S(2)}, u32[]{:S(2)}) collective-permute-start(f32[512,512]{1,0:T(8,128)} %convolution_add_fusion.3), channel_id=1, source_target_pairs={{0,16},{2,20},{4,22},{6,24},{8,26},{10,28},{12,30},{14,31},{16,32}... | collective-permute-start | bytes 3145736 | tf_op jit(solution)/shard_map/ppermute | solution.py:73
  112.1 36.9 %collective-permute-start.29 = (f32[512,512]{1,0:T(8,128)S(1)}, f32[512,512]{1,0:T(8,128)}, u32[]{:S(2)}, u32[]{:S(2)}) collective-permute-start(f32[512,512]{1,0:T(8,128)S(1)} %convolution_add_fusion.2), channel_id=1, source_target_pairs={{1,18},{3,17},{5,19},{7,21},{9,23},{11,25},{13,27},{15,29},{16,0},... | collective-permute-start | bytes 3145736 | tf_op jit(solution)/shard_map/ppermute | solution.py:73
  144.7 19.5 %collective-permute-start.27 = (f32[512,512]{1,0:T(8,128)}, f32[512,512]{1,0:T(8,128)}, u32[]{:S(2)}, u32[]{:S(2)}) collective-permute-start(f32[512,512]{1,0:T(8,128)} %collective-permute-done.26), channel_id=1, source_target_pairs={{72,64},{56,48},{70,79},{54,63}} | collective-permute-start | bytes 3145736 | tf_op jit(solution)/shard_map/ppermute | solution.py:73
  170.0 38.8 %collective-permute-start.38 = (f32[1024,512]{1,0:T(8,128)S(1)}, f32[1024,512]{1,0:T(8,128)S(1)}, u32[]{:S(2)}, u32[]{:S(2)}) collective-permute-start(f32[1024,512]{1,0:T(8,128)S(1)} %fusion), channel_id=1, source_target_pairs={{0,1},{1,0},{2,3},{3,2},{4,5},{5,4},{6,7},{7,6},{8,9},{9,8},{10,11... | collective-permute-start | bytes 6291464 | tf_op jit(solution)/shard_map/ppermute | solution.py:73
  170.1 13.9 %collective-permute-start.30 = (f32[128,512]{1,0:T(8,128)S(1)}, f32[128,512]{1,0:T(8,128)S(1)}, u32[]{:S(2)}, u32[]{:S(2)}) collective-permute-start(f32[128,512]{1,0:T(8,128)S(1)} %pad_maximum_fusion.1.refs_0_), channel_id=1, source_target_pairs={{0,0},{1,1},{2,16},{3,17},{4,32},{5,33},{6,48},{7,49},{8,64},{9,65... | collective-permute-start | bytes 786440 | tf_op jit(solution)/shard_map/ppermute | solution.py:73
  184.0 10.7 %collective-permute-start.32 = (f32[128,512]{1,0:T(8,128)S(1)}, f32[128,512]{1,0:T(8,128)S(1)}, u32[]{:S(2)}, u32[]{:S(2)}) collective-permute-start(f32[128,512]{1,0:T(8,128)S(1)} %collective-permute-done.30.refs_0_), channel_id=1, source_target_pairs={{0,32},{1,33},{2,34},{3,35},{4,36},{5,37},{6,38},{7,39},{8,40},{9,... | collective-permute-start | bytes 786440 | tf_op jit(solution)/shard_map/ppermute | solution.py:73
  184.0 15.1 %collective-permute-start.31 = (f32[128,512]{1,0:T(8,128)S(1)}, f32[128,512]{1,0:T(8,128)S(1)}, u32[]{:S(2)}, u32[]{:S(2)}) collective-permute-start(f32[128,512]{1,0:T(8,128)S(1)} %collective-permute-done.30.refs_0_), channel_id=1, source_target_pairs={{0,48},{1,49},{2,50},{3,51},{4,52},{5,53},{6,54},{7,55},{8,56},{9,... | collective-permute-start | bytes 786440 | tf_op jit(solution)/shard_map/ppermute | solution.py:73
  184.4 16.5 %collective-permute-start.33 = (f32[128,512]{1,0:T(8,128)S(1)}, f32[128,512]{1,0:T(8,128)S(1)}, u32[]{:S(2)}, u32[]{:S(2)}) collective-permute-start(f32[128,512]{1,0:T(8,128)S(1)} %collective-permute-done.30.refs_0_), channel_id=1, source_target_pairs={{0,16},{1,17},{2,18},{3,19},{4,20},{5,21},{6,22},{7,23},{8,24},{9,... | collective-permute-start | bytes 786440 | tf_op jit(solution)/shard_map/ppermute | solution.py:73
  193.4 10.9 %collective-permute-start.35 = (f32[128,512]{1,0:T(8,128)S(1)}, f32[128,512]{1,0:T(8,128)S(1)}, u32[]{:S(2)}, u32[]{:S(2)}) collective-permute-start(f32[128,512]{1,0:T(8,128)S(1)} %collective-permute-done.34.refs_4_), channel_id=1, source_target_pairs={{0,48},{1,49},{2,50},{3,51},{4,52},{5,53},{6,54},{7,55},{8,56},{9,... | collective-permute-start | bytes 786440 | tf_op jit(solution)/shard_map/ppermute | solution.py:73
  211.1 41.8 %collective-permute-start.39 = (f32[512,512]{1,0:T(8,128)S(1)}, f32[512,512]{1,0:T(8,128)S(1)}, u32[]{:S(2)}, u32[]{:S(2)}) collective-permute-start(f32[512,512]{1,0:T(8,128)S(1)} %broadcast_select_fusion.4), channel_id=1, source_target_pairs={{0,0},{1,2},{2,4},{3,1},{4,6},{5,3},{6,8},{7,5},{8,10},{9,7},{10,1... | collective-permute-start | bytes 3145736 | tf_op jit(solution)/shard_map/ppermute | solution.py:73
  217.8 37.0 %collective-permute-start.41 = (f32[512,512]{1,0:T(8,128)S(1)}, f32[512,512]{1,0:T(8,128)S(1)}, u32[]{:S(2)}, u32[]{:S(2)}) collective-permute-start(f32[512,512]{1,0:T(8,128)S(1)} %convolution_add_fusion.1), channel_id=1, source_target_pairs={{0,16},{2,20},{4,22},{6,24},{8,26},{10,28},{12,30},{14,31},{16,32}... | collective-permute-start | bytes 3145736 | tf_op jit(solution)/shard_map/ppermute | solution.py:73
  219.1 35.7 %collective-permute-start.42 = (f32[512,512]{1,0:T(8,128)S(1)}, f32[512,512]{1,0:T(8,128)S(1)}, u32[]{:S(2)}, u32[]{:S(2)}) collective-permute-start(f32[512,512]{1,0:T(8,128)S(1)} %convolution_add_fusion), channel_id=1, source_target_pairs={{1,18},{3,17},{5,19},{7,21},{9,23},{11,25},{13,27},{15,29},{16,0},... | collective-permute-start | bytes 3145736 | tf_op jit(solution)/shard_map/ppermute | solution.py:73
  252.9 16.7 %collective-permute-start.40 = (f32[512,512]{1,0:T(8,128)S(1)}, f32[512,512]{1,0:T(8,128)S(1)}, u32[]{:S(2)}, u32[]{:S(2)}) collective-permute-start(f32[512,512]{1,0:T(8,128)S(1)} %collective-permute-done.39), channel_id=1, source_target_pairs={{72,64},{56,48},{70,79},{54,63}} | collective-permute-start | bytes 3145736 | tf_op jit(solution)/shard_map/ppermute | solution.py:73
  (20 other events, 126.7 us)
